TPU v7x, 32 devices: a whole 2x2x4 slice. The times are simulated.
32 devices in a mesh: dp: 2 (over y), ctx: 4 (over z), exp: 4 (over x, core).
Axes of the slice: x: 2, y: 2, z: 4, core: 2. Of those that a mesh axis runs over, the one named last changes fastest.
Arguments:
- queries: bfloat16 [8, 512, 2048], P(('dp', 'exp'), 'ctx'), may hold values from -24 to 24
- keys: bfloat16 [8, 512, 2048], P(('dp', 'exp'), 'ctx'), may hold values from -20 to 20
- values: bfloat16 [8, 512, 2048], P(('dp', 'exp'), 'ctx'), may hold values from -6 to 6
- resid: bfloat16 [8, 512, 2048], P(('dp', 'exp'), 'ctx'), may hold values from -3 to 3
- norm_gain: float32 [2048], replicated, may hold values from 0.5 to 1.5
- expert_ids: int32 [8, 512, 8], P(('dp', 'exp'), 'ctx'), may hold values from 0 to 15, all different within a row; in each aligned block of 128 rows (0 to 127, 128 to 255, ..., all dimensions but the last counted through in order) at most 68 rows name the same one
- gate_weights: float32 [8, 512, 8], P(('dp', 'exp'), 'ctx'), may hold values from 0.05 to 0.5
- mask_flags: int32 [8, 512], P(('dp', 'exp'), 'ctx'), may hold values 0 or 1
- cotangent: bfloat16 [8, 512, 2048], P(('dp', 'exp'), 'ctx'), may hold values from -0.59765625 to 0.59765625
- w_gate_up: bfloat16 [16, 2048, 1024], P(('ctx', 'exp')), may hold values from -0.125 to 0.125
- w_down: bfloat16 [16, 2048, 512], P(('ctx', 'exp')), may hold values from -0.25 to 0.25
Outputs:
- stream: bfloat16 [8, 512, 2048], P(('dp', 'exp'), 'ctx')
- grad_gate_up: float32 [16, 2048, 1024], P(('ctx', 'exp'), 'dp')
- grad_down: float32 [16, 2048, 512], P(('ctx', 'exp'), 'dp')
Inputs may be any that keep to these rules, and one draw needn't show every extreme that they name: `expert_ids`: in the rows of one device no expert is named more than 68 times, and some device names some expert exactly 68 times.
All inputs are finite; a program needn't handle non-finite values. No bound on the sum of `mask_flags` on one device may be relied on, other than what follows from the above.
Results may differ from a plain program's by a relative error of at most 0.0088.
Values may be sent and summed in bfloat16 or wider, within the bound.
No kernel may reach another device: no remote copies, remote signals or barrier semaphores. Data moves between devices by JAX's collectives and lax.ppermute only.
A program may use at most 128 MiB of HBM per device.

v0:
```python
import math
import jax
import jax.numpy as jnp
from jax import lax
from jax.sharding import PartitionSpec as P

HEADS = 16
HEAD_DIM = 128


def attend(query_rows, keys_all, values_all):
    tokens = query_rows.shape[0]
    length = keys_all.shape[0]
    query_heads = query_rows.reshape(tokens, HEADS, HEAD_DIM)
    key_heads = keys_all.reshape(length, HEADS, HEAD_DIM)
    value_heads = values_all.reshape(length, HEADS, HEAD_DIM)
    scale_factor = 1.0 / math.sqrt(HEAD_DIM)
    scores = (
        jnp.einsum("qhd,khd->hqk", query_heads, key_heads, preferred_element_type=jnp.float32)
        * scale_factor
    )
    largest = jnp.max(scores, axis=2, keepdims=True)
    powers = jnp.exp(scores - largest)
    probs = (powers / jnp.sum(powers, axis=2, keepdims=True)).astype(jnp.bfloat16)
    attended = jnp.einsum("hqk,khd->qhd", probs, value_heads, preferred_element_type=jnp.float32)
    return attended.reshape(tokens, HEADS * HEAD_DIM)


def rms_normed(stream, norm_gain):
    widened = lax.optimization_barrier(stream).astype(jnp.float32)
    factor = lax.rsqrt(jnp.mean(widened * widened, axis=-1, keepdims=True) + 1e-05)
    return (widened * factor * norm_gain).astype(jnp.bfloat16)


def slot_targets(routes, experts, capacity):
    flat_ids = routes.reshape(-1)
    onehot = (flat_ids[:, None] == jnp.arange(experts, dtype=jnp.int32)[None, :]).astype(jnp.int32)
    ranks = jnp.cumsum(onehot, axis=0) - 1
    within = jnp.sum(ranks * onehot, axis=1)
    return flat_ids * capacity + within


def pack_rows(normed, cot_rows, routes, gates, flags, experts, capacity):
    tokens = normed.shape[0]
    model_width = normed.shape[1]
    top_count = routes.shape[1]
    targets = slot_targets(routes, experts, capacity)
    scaled = (
        cot_rows.astype(jnp.float32)[:, None, :]
        * gates[:, :, None]
        * flags.astype(jnp.float32)[:, None, None]
    )
    grad_rows = scaled.astype(jnp.bfloat16).reshape(tokens * top_count, model_width)
    input_rows = jnp.repeat(normed, top_count, axis=0)
    empty = jnp.zeros((experts * capacity, model_width), jnp.bfloat16)
    return (empty.at[targets].set(input_rows), empty.at[targets].set(grad_rows))


def expert_term(input_rows, grad_rows, gate_up, down_map):
    hidden_width = down_map.shape[1]
    projected = jnp.dot(input_rows, gate_up, preferred_element_type=jnp.float32)
    gate_part = projected[:, :hidden_width]
    up_part = projected[:, hidden_width:]
    sigma = jax.nn.sigmoid(gate_part)
    activated = gate_part * sigma
    hidden = (activated * up_part).astype(jnp.bfloat16)
    back_hidden = jnp.dot(grad_rows, down_map, preferred_element_type=jnp.float32)
    slope = sigma * (1.0 + gate_part * (1.0 - sigma))
    back_both = jnp.concatenate(
        [back_hidden * up_part * slope, back_hidden * activated], axis=1
    ).astype(jnp.bfloat16)
    return (hidden, back_both)


def term_rows(input_rows, grad_rows, hidden, back_both):
    contract = (((0,), (0,)), ((), ()))
    left_part = lax.dot_general(input_rows, back_both, contract, preferred_element_type=jnp.float32)
    right_part = lax.dot_general(grad_rows, hidden, contract, preferred_element_type=jnp.float32)
    return jnp.concatenate([left_part, right_part], axis=1)


def per_device(
    queries,
    keys,
    values,
    resid,
    norm_gain,
    expert_ids,
    gate_weights,
    mask_flags,
    cotangent,
    w_gate_up,
    w_down,
):
    keys_all, values_all = (
        lax.all_gather(keys, "ctx", axis=1, tiled=True),
        lax.all_gather(values, "ctx", axis=1, tiled=True),
    )
    attended = attend(queries[0], keys_all[0], values_all[0])
    stream = (resid[0].astype(jnp.float32) + attended).astype(jnp.bfloat16)
    normed = rms_normed(stream, norm_gain)
    ctx_count = lax.axis_size("ctx")
    exp_count = lax.axis_size("exp")
    experts = ctx_count * exp_count
    tokens = queries.shape[1]
    capacity = min(tokens, tokens * expert_ids.shape[2] * 17 // (16 * experts))
    model_width = normed.shape[1]
    input_buf, grad_buf = pack_rows(
        normed, cotangent[0], expert_ids[0], gate_weights[0], mask_flags[0], experts, capacity
    )
    block_shape = (experts, capacity, model_width)
    arrived = (
        lax.all_to_all(
            input_buf.reshape(block_shape), ("ctx", "exp"), split_axis=0, concat_axis=0, tiled=True
        ),
        lax.all_to_all(
            grad_buf.reshape(block_shape), ("ctx", "exp"), split_axis=0, concat_axis=0, tiled=True
        ),
    )
    input_rows = arrived[0].reshape(-1, model_width)
    grad_rows = arrived[1].reshape(-1, model_width)
    hidden, back_both = expert_term(input_rows, grad_rows, w_gate_up[0], w_down[0])
    summed = lax.psum_scatter(
        term_rows(input_rows, grad_rows, hidden, back_both).astype(jnp.bfloat16),
        "dp",
        scatter_dimension=0,
        tiled=True,
    ).astype(jnp.float32)
    hidden_width = w_down.shape[2]
    return (stream[None], summed[:, : 2 * hidden_width][None], summed[:, 2 * hidden_width :][None])


def solution(mesh):
    placed = (
        P(("dp", "exp"), "ctx", None),
        P(("dp", "exp"), "ctx", None),
        P(("dp", "exp"), "ctx", None),
        P(("dp", "exp"), "ctx", None),
        P(),
        P(("dp", "exp"), "ctx", None),
        P(("dp", "exp"), "ctx", None),
        P(("dp", "exp"), "ctx"),
        P(("dp", "exp"), "ctx", None),
        P(("ctx", "exp"), None, None),
        P(("ctx", "exp"), None, None),
    )
    return jax.shard_map(
        per_device,
        mesh=mesh,
        in_specs=placed,
        out_specs=(
            P(("dp", "exp"), "ctx", None),
            P(("ctx", "exp"), "dp", None),
            P(("ctx", "exp"), "dp", None),
        ),
        check_vma=False,
    )
```

profile of v0, /device:TPU:0, one launch (start us, length us, event | category | flops | bytes accessed | tf_op | source)
XLA Modules:
  0.0 449.8 jit_solution(16724601727391645695)
XLA Ops:
  7.2 0.7 all-gather.5.cloned.1.call-update
  7.9 0.7 broadcast_multiply_fusion
  8.6 0.8 copy.28
  9.6 0.7 convert_bitcast_fusion.1
  10.2 0.1 copy.27
  10.3 0.1 mul.100
  10.6 4.5 %reduce-window.6 = s32[16,8,128]{2,1,0:T(8,128)S(1)} reduce-window(s32[16,8,128]{2,1,0:T(8,128)S(1)} %fusion.37, s32[]{:T(128)} %constant.8.clone.1), window={size=1x1x128 pad=0_0x0_0x127_0}, to_apply=%region_2.0 | reduce-window | flops 2080768 | bytes 131076 | tf_op jit(solution)/shard_map/reduce-window
  15.2 0.1 copy.30
  15.6 0.8 copy.33
  16.4 1.1 bitcast_convert_fusion
  17.6 9.7 %scatter_custom_fusion.1 = bf16[1088,2048]{1,0:T(8,128)(2,1)} fusion(s32[1024]{0:T(1024)S(1)} %bitcast.80, f32[1024]{0:T(1024)S(1)} %mul.113, f32[1024]{0:T(1024)S(1)} %mul.109, f32[128,2048]{1,0:T(8,128)S(1)} %bitcast_convert_fusion, bf16[]{:T(256)} %constant.6.clone.1), kind=kCustom, calls=%fused_computation.7 | custom fusion | flops 6291456 | bytes 5513218 | tf_op jit(solution)/shard_map/scatter | solution.py:56
  27.3 7.1 %reshape.112 = bf16[16,68,2048]{2,1,0:T(8,128)(2,1)} reshape(bf16[1088,2048]{1,0:T(8,128)(2,1)} %scatter_custom_fusion.1) | data formatting | bytes 8912896 | tf_op jit(solution)/shard_map/reshape | solution.py:117
  34.4 7.6 %all-to-all-start.1 = ((bf16[16,68,2048]{2,1,0:T(8,128)(2,1)}), bf16[16,68,2048]{2,1,0:T(8,128)(2,1)}, u32[]{:S(2)}, u32[]{:S(2)}) async-start(bf16[16,68,2048]{2,1,0:T(8,128)(2,1)} %reshape.112), calls=%async_computation.1 | async-start | bytes 9437184 | tf_op jit(solution)/shard_map/all_to_all | solution.py:116
  42.0 0.2 all-gather.3.cloned.1.call-start
  42.2 1.0 copy.22
  43.3 0.1 copy.37
  43.4 46.5 %all-gather.5.cloned.1.call-done = bf16[1,512,2048]{2,1,0:T(8,128)(2,1)} async-done(((bf16[1,128,2048]{2,1,0:T(8,128)(2,1)}), bf16[1,512,2048]{2,1,0:T(8,128)(2,1)}) %all-gather.5.cloned.1.call-update) | async-done | bytes 2097168 | tf_op jit(solution)/shard_map/all_gather | solution.py:97
  89.9 3.9 copy.25
  93.8 78.7 %all-gather.3.cloned.1.call-done = bf16[1,512,2048]{1,2,0:T(8,128)(2,1)} async-done(((bf16[1,128,2048]{1,2,0:T(8,128)(2,1)}), bf16[1,512,2048]{1,2,0:T(8,128)(2,1)}) %all-gather.3.cloned.1.call-update) | async-done | bytes 2097168 | tf_op jit(solution)/shard_map/all_gather | solution.py:96
  172.5 2.3 fusion.32
  174.8 1.4 fusion.48
  176.2 0.6 copy-done.2
  176.8 7.9 %fusion.25 = f32[16,128,128]{1,2,0:T(8,128)S(1)} fusion(bf16[512,16,128]{0,2,1:T(8,128)(2,1)} %bitcast.74, f32[16,128]{1,0:T(8,128)S(1)} %fusion.48, f32[16,128,512]{2,1,0:T(8,128)} %copy-done.2), kind=kOutput, calls=%fused_computation.37 | convolution fusion | flops 273680896 | bytes 7348224 | tf_op jit(solution)/shard_map/hqk,khd->qhd/dot_general | solution.py:25
  184.8 1.3 copy.32
  186.1 1.5 fusion.28
  187.5 0.2 fusion.29
  187.7 1.0 fusion.31
  188.7 9.6 %scatter_custom_fusion = bf16[1088,2048]{1,0:T(8,128)(2,1)} fusion(s32[1024]{0:T(1024)S(1)} %bitcast.81, bf16[]{:T(256)} %constant.6.clone.1, bf16[128,2048]{1,0:T(8,128)(2,1)} %fusion.31), kind=kCustom, calls=%fused_computation.11 | custom fusion | bytes 4980738 | tf_op jit(solution)/shard_map/scatter | solution.py:56
  198.4 7.0 %reshape.110 = bf16[16,68,2048]{2,1,0:T(8,128)(2,1)} reshape(bf16[1088,2048]{1,0:T(8,128)(2,1)} %scatter_custom_fusion) | data formatting | bytes 8912896 | tf_op jit(solution)/shard_map/reshape | solution.py:114
  205.4 9.0 %all-to-all-start = ((bf16[16,68,2048]{2,1,0:T(8,128)(2,1)}), bf16[16,68,2048]{2,1,0:T(8,128)(2,1)}, u32[]{:S(2)}, u32[]{:S(2)}) async-start(bf16[16,68,2048]{2,1,0:T(8,128)(2,1)} %reshape.110), calls=%async_computation | async-start | bytes 9437184 | tf_op jit(solution)/shard_map/all_to_all | solution.py:113
  214.3 0.3 reduce-scatter.2.cloned.1.call-start
  214.6 7.1 %reshape.113 = bf16[1088,2048]{1,0:T(8,128)(2,1)} reshape(bf16[16,68,2048]{2,1,0:T(8,128)(2,1)} %all-to-all-done.1) | data formatting | bytes 8912896 | tf_op jit(solution)/shard_map/reshape | solution.py:121
  221.7 79.4 %all-to-all-done = bf16[16,68,2048]{2,1,0:T(8,128)(2,1)} async-done(((bf16[16,68,2048]{2,1,0:T(8,128)(2,1)}), bf16[16,68,2048]{2,1,0:T(8,128)(2,1)}, u32[]{:S(2)}, u32[]{:S(2)}) %all-to-all-start) | async-done | bytes 4456480 | tf_op jit(solution)/shard_map/all_to_all | solution.py:113
  301.2 7.1 %reshape.111 = bf16[1088,2048]{1,0:T(8,128)(2,1)} reshape(bf16[16,68,2048]{2,1,0:T(8,128)(2,1)} %all-to-all-done) | data formatting | bytes 8912896 | tf_op jit(solution)/shard_map/reshape | solution.py:120
  308.2 8.0 %fusion.5 = f32[1088,1024]{1,0:T(8,128)S(1)} fusion(bf16[1088,2048]{1,0:T(8,128)(2,1)} %reshape.111, bf16[1,2048,1024]{2,1,0:T(8,128)(2,1)} %param.20), kind=kOutput, calls=%fused_computation.9 | convolution fusion | flops 4563402752 | bytes 13107200 | tf_op jit(solution)/shard_map/dot_general | solution.py:61
  316.3 4.3 convolution_convert_fusion.1
  320.6 3.3 multiply_convert_fusion.2
  323.9 6.2 %convolution_convert_fusion = bf16[2048,1024]{0,1:T(8,128)(2,1)S(1)} fusion(bf16[1088,2048]{1,0:T(8,128)(2,1)S(1)} %bitcast.70, bf16[1088,512]{1,0:T(8,128)(2,1)S(1)} %get-tuple-element.10, bf16[1088,512]{1,0:T(8,128)(2,1)S(1)} %get-tuple-element.9), kind=kOutput, calls=%fused_computation.18 | convolution fusion | flops 4569956352 | bytes 10878976 | tf_op jit(solution)/shard_map/dot_general | solution.py:77
  330.2 3.7 pad_maximum_fusion
  333.9 0.3 copy.26
  334.3 0.7 copy-done.4
  334.9 0.9 fusion.26
  335.8 92.3 %reduce-scatter.2.cloned.1.call-done = bf16[1024,1536]{0,1:T(8,128)(2,1)} async-done(((bf16[2048,1536]{0,1:T(8,128)(2,1)}), bf16[1024,1536]{0,1:T(8,128)(2,1)}) %reduce-scatter.2.cloned.1.call-update) | async-done | bytes 3145744 | tf_op jit(solution)/shard_map/reduce_scatter | solution.py:123
  428.1 2.6 convert_element_type.76
  430.8 1.6 slice_bitcast_fusion.1
  432.3 2.5 slice_bitcast_fusion
  434.9 5.5 %copy.34 = f32[1,1024,1024]{2,1,0:T(8,128)} copy(f32[1,1024,1024]{1,2,0:T(8,128)} %slice_bitcast_fusion) | data formatting | bytes 8388608
  440.3 2.9 copy.35
  (42 shorter events, 0.9 us)
Async XLA Ops:
  7.2 313.4 %copy-start = (bf16[1,2048,512]{2,1,0:T(8,128)(2,1)S(1)}, bf16[1,2048,512]{2,1,0:T(8,128)(2,1)}, u32[]{:S(2)}) copy-start(bf16[1,2048,512]{2,1,0:T(8,128)(2,1)} %param.21) | copy-start | bytes 6291460
  7.2 82.7 %all-gather.5.cloned.1.call-start = ((), (), s32[]{:S(2)}) async-start(), calls=%async_computation.4 | async-start | bytes 2621440 | tf_op jit(solution)/shard_map/all_gather | solution.py:97
  34.4 7.8 %copy-start.5 = (bf16[1,128,2048]{2,1,0:T(8,128)(2,1)S(1)}, bf16[1,128,2048]{2,1,0:T(8,128)(2,1)}, u32[]{:S(2)}) copy-start(bf16[1,128,2048]{2,1,0:T(8,128)(2,1)} %param.12) | copy-start | bytes 1572868
  34.4 8.8 %copy-start.6 = (bf16[1,128,2048]{2,1,0:T(8,128)(2,1)S(1)}, bf16[1,128,2048]{2,1,0:T(8,128)(2,1)}, u32[]{:S(2)}) copy-start(bf16[1,128,2048]{2,1,0:T(8,128)(2,1)} %param.11) | copy-start | bytes 1572868
  34.4 170.9 %all-to-all-start.1 = ((bf16[16,68,2048]{2,1,0:T(8,128)(2,1)}), bf16[16,68,2048]{2,1,0:T(8,128)(2,1)}, u32[]{:S(2)}, u32[]{:S(2)}) async-start(bf16[16,68,2048]{2,1,0:T(8,128)(2,1)} %reshape.112), calls=%async_computation.1 | async-start | bytes 9437184 | tf_op jit(solution)/shard_map/all_to_all | solution.py:116
  42.0 130.5 %all-gather.3.cloned.1.call-start = ((), (), s32[]{:S(2)}) async-start(), calls=%async_computation.3 | async-start | bytes 2621440 | tf_op jit(solution)/shard_map/all_gather | solution.py:96
  174.8 2.0 copy-start.2
  184.7 3.0 copy-start.7
  205.4 95.8 %all-to-all-start = ((bf16[16,68,2048]{2,1,0:T(8,128)(2,1)}), bf16[16,68,2048]{2,1,0:T(8,128)(2,1)}, u32[]{:S(2)}, u32[]{:S(2)}) async-start(bf16[16,68,2048]{2,1,0:T(8,128)(2,1)} %reshape.110), calls=%async_computation | async-start | bytes 9437184 | tf_op jit(solution)/shard_map/all_to_all | solution.py:113
  214.3 213.8 %reduce-scatter.2.cloned.1.call-start = ((), (), s32[]{:S(2)}) async-start(), calls=%async_computation.5 | async-start | bytes 9437184 | tf_op jit(solution)/shard_map/reduce_scatter | solution.py:123
  301.1 15.1 %slice-start = ((s8[4456448]{0:T(1024)(128)(4,1)}), s8[262144]{0:T(1024)(128)(4,1)S(1)}, s32[]{:S(2)}) async-start(s8[4456448]{0:T(1024)(128)(4,1)} %bitcast.67), calls=%async_computation.6 | async-start | bytes 524288
  308.2 8.0 %slice-start.1 = ((s8[4456448]{0:T(1024)(128)(4,1)}), s8[4194304]{0:T(1024)(128)(4,1)S(1)}, s32[]{:S(2)}) async-start(s8[4456448]{0:T(1024)(128)(4,1)} %bitcast.67), calls=%async_computation.7 | async-start | bytes 8388608
  316.2 7.6 %slice-start.2 = ((s8[4456448]{0:T(1024)(128)(4,1)}), s8[4194304]{0:T(1024)(128)(4,1)S(1)}, s32[]{:S(2)}) async-start(s8[4456448]{0:T(1024)(128)(4,1)} %bitcast.69), calls=%async_computation.8 | async-start | bytes 8388608
  320.6 3.3 slice-start.3
  323.9 6.3 %copy-start.3 = (bf16[2048,512]{0,1:T(8,128)(2,1)S(1)}, bf16[2048,512]{0,1:T(8,128)(2,1)}, u32[]{:S(2)}) copy-start(bf16[2048,512]{0,1:T(8,128)(2,1)} %convolution_convert_fusion.1) | copy-start | bytes 6291460
  333.9 1.0 copy-start.4
  434.9 8.4 %copy-start.1 = (bf16[1,2048,512]{2,1,0:T(8,128)(2,1)S(1)}, bf16[1,2048,512]{2,1,0:T(8,128)(2,1)}, u32[]{:S(2)}) copy-start(bf16[1,2048,512]{2,1,0:T(8,128)(2,1)} %param.21) | copy-start | bytes 6291460
Sparse Core Ops, SparseCore 0:
  9.6 80.2 all-gather.4
  92.0 80.4 all-gather.2
  334.0 94.0 reduce-scatter.1
where the time goes:
time: 451 us; the launch traced here: 450 us
  waiting for transfers between devices  298 us (66%)
  local copies, waits for them, and re-layouts  61 us (14%)
  matrix products  32 us (7%)
  other arithmetic  28.1 us (6%)
  starting transfers between devices  17 us (4%)
  between operations  14 us (3%)
    reduce_scatter x1, waiting for transfers between devices, per_device(): lax.psum_scatter(term_rows(input_rows, grad_rows, hidden, back_both).asty...  92.3 us
    all_to_all x1, waiting for transfers between devices, per_device(): lax.all_to_all(input_buf.reshape(block_shape), ('ctx', 'exp'), split_axis...  79.4 us
    all_gather x1, waiting for transfers between devices, per_device(): lax.all_gather(keys, 'ctx', axis=1, tiled=True)  78.7 us
    all_gather x1, waiting for transfers between devices, per_device(): lax.all_gather(values, 'ctx', axis=1, tiled=True)  46.5 us
    unnamed x30, local copies, waits for them, and re-layouts  12.4 us
    scatter x1, other arithmetic, pack_rows(): return (empty.at[targets].set(input_rows), empty.at[targets].set(grad_rows))  9.65 us
    scatter x1, local copies, waits for them, and re-layouts, pack_rows(): return (empty.at[targets].set(input_rows), empty.at[targets].set(grad_rows))  9.63 us
  transfers between devices with their start and end apart: 5, of which 4 were waited for; matrix products, arithmetic and copies ran while one was open for 16% of the time, Pallas kernels for 0%

commit v1 on v0

--- a/solution.py
+++ b/solution.py
@@ -6,6 +6,24 @@
 
 HEADS = 16
 HEAD_DIM = 128
+
+
+def collect(shard, axis, dim):
+    ways, here, hop = (lax.axis_size(axis), lax.axis_index(axis), shard.shape[dim])
+    lengths = [n * ways if d == dim else n for d, n in enumerate(shard.shape)]
+    full = lax.dynamic_update_slice_in_dim(
+        jnp.zeros(lengths, shard.dtype), shard, here * hop, axis=dim
+    )
+    going_up = going_down = shard
+    for far in range(1, ways // 2 + 1):
+        going_up = lax.ppermute(going_up, axis, [(d, (d + 1) % ways) for d in range(ways)])
+        full = lax.dynamic_update_slice_in_dim(full, going_up, (here - far) % ways * hop, axis=dim)
+        if 2 * far < ways:
+            going_down = lax.ppermute(going_down, axis, [(d, (d - 1) % ways) for d in range(ways)])
+            full = lax.dynamic_update_slice_in_dim(
+                full, going_down, (here + far) % ways * hop, axis=dim
+            )
+    return full
 
 
 def attend(query_rows, keys_all, values_all):
@@ -93,7 +111,7 @@
     w_down,
 ):
     keys_all, values_all = (
-        lax.all_gather(keys, "ctx", axis=1, tiled=True),
+        collect(keys, "ctx", 1),
         lax.all_gather(values, "ctx", axis=1, tiled=True),
     )
     attended = attend(queries[0], keys_all[0], values_all[0])

time: 451 us -> 495 us (1.098)
  starting transfers between devices: 17 us -> 52.1 us
  local copies, waits for them, and re-layouts: 61 us -> 70.5 us
    ppermute x0 -> x3, waiting for transfers between devices: none -> 126 us  [the longest x2 126 us: collect(): lax.ppermute(going_up, axis, [(d, (d + 1) % ways) for d in range(ways)])]
    all_gather x1 -> x0, waiting for transfers between devices: 78.7 us -> none  [per_device(): lax.all_gather(keys, 'ctx', axis=1, tiled=True)]
    all_gather x1, waiting for transfers between devices: 46.5 us -> 0.01 us  [per_device(): lax.all_gather(values, 'ctx', axis=1, tiled=True)]
    ppermute x0 -> x3, starting transfers between devices: none -> 37.4 us  [the longest x2 35.5 us: collect(): lax.ppermute(going_up, axis, [(d, (d + 1) % ways) for d in range(ways)])]
    dynamic_update_slice x0 -> x4, local copies, waits for them, and re-layouts: none -> 6.44 us  [the longest x2 3.74 us: collect(): lax.dynamic_update_slice_in_dim(full, going_up, (here - far) % ways * hop...]
    unnamed x30 -> x28, local copies, waits for them, and re-layouts: 12.4 us -> 14.1 us
  transfers between devices with their start and end apart: 5 -> 7, of which waited for: 4 -> 4; matrix products, arithmetic and copies ran while one was open for 16% -> 10% of each run, Pallas kernels for 0% -> 0%
where the time goes in v1:
time: 495 us; the launch traced here: 493 us
  waiting for transfers between devices  298 us (60%)
  local copies, waits for them, and re-layouts  70.5 us (14%)
  starting transfers between devices  52.1 us (11%)
  matrix products  30.1 us (6%)
  other arithmetic  27.9 us (6%)
  between operations  14.3 us (3%)
    ppermute x2, waiting for transfers between devices, collect(): lax.ppermute(going_up, axis, [(d, (d + 1) % ways) for d in range(ways)])  126 us
    reduce_scatter x1, waiting for transfers between devices, per_device(): lax.psum_scatter(term_rows(input_rows, grad_rows, hidden, back_both).asty...  92.4 us
    all_to_all x1, waiting for transfers between devices, per_device(): lax.all_to_all(input_buf.reshape(block_shape), ('ctx', 'exp'), split_axis...  79.5 us
    ppermute x2, starting transfers between devices, collect(): lax.ppermute(going_up, axis, [(d, (d + 1) % ways) for d in range(ways)])  35.5 us
    unnamed x28, local copies, waits for them, and re-layouts  14.1 us
  transfers between devices with their start and end apart: 7, of which 4 were waited for; matrix products, arithmetic and copies ran while one was open for 10% of the time, Pallas kernels for 0%

profile of v1, /device:TPU:0, one launch (start us, length us, event | category | flops | bytes accessed | tf_op | source)
XLA Modules:
  0.0 493.1 jit_solution(18416686503206618369)
XLA Ops:
  7.2 0.8 broadcast_multiply_fusion
  8.0 0.8 copy.32
  9.0 0.7 convert_bitcast_fusion.1
  10.0 4.5 reduce-window.6
  15.0 0.8 copy.37
  15.9 1.1 bitcast_convert_fusion
  17.1 9.7 %scatter_custom_fusion.1 = bf16[1088,2048]{1,0:T(8,128)(2,1)} fusion(s32[1024]{0:T(1024)S(1)} %bitcast.98, f32[1024]{0:T(1024)S(1)} %mul.133, f32[1024]{0:T(1024)S(1)} %mul.129, f32[128,2048]{1,0:T(8,128)S(1)} %bitcast_convert_fusion, bf16[]{:T(256)} %constant.46.clone.1), kind=kCustom, calls=%fused_computation.7 | custom fusion | flops 6291456 | bytes 5513218 | tf_op jit(solution)/shard_map/scatter | solution.py:74
  26.7 7.1 %reshape.112 = bf16[16,68,2048]{2,1,0:T(8,128)(2,1)} reshape(bf16[1088,2048]{1,0:T(8,128)(2,1)} %scatter_custom_fusion.1) | data formatting | bytes 8912896 | tf_op jit(solution)/shard_map/reshape | solution.py:135
  33.8 7.5 %all-to-all-start.1 = ((bf16[16,68,2048]{2,1,0:T(8,128)(2,1)}), bf16[16,68,2048]{2,1,0:T(8,128)(2,1)}, u32[]{:S(2)}, u32[]{:S(2)}) async-start(bf16[16,68,2048]{2,1,0:T(8,128)(2,1)} %reshape.112), calls=%async_computation.1 | async-start | bytes 9437184 | tf_op jit(solution)/shard_map/all_to_all | solution.py:134
  41.4 0.7 all-gather.2.cloned.1.call-update
  42.4 1.9 collective-permute-start
  44.3 2.0 collective-permute-start.1
  46.3 121.5 %collective-permute-done = bf16[1,128,2048]{1,2,0:T(8,128)(2,1)} collective-permute-done((bf16[1,128,2048]{1,2,0:T(8,128)(2,1)S(1)}, bf16[1,128,2048]{1,2,0:T(8,128)(2,1)}, u32[]{:S(2)}, u32[]{:S(2)}) %collective-permute-start) | collective-permute-done | bytes 524320 | tf_op jit(solution)/shard_map/ppermute | solution.py:19
  167.8 33.5 %collective-permute-start.2 = (bf16[1,128,2048]{1,2,0:T(8,128)(2,1)}, bf16[1,128,2048]{1,2,0:T(8,128)(2,1)}, u32[]{:S(2)}, u32[]{:S(2)}) collective-permute-start(bf16[1,128,2048]{1,2,0:T(8,128)(2,1)} %collective-permute-done), channel_id=1, source_target_pairs={{0,4},{4,8},{8,12},{12,0},{1,5},{5,9},{9,13},{13,1},{2,6},{6,10},{... | collective-permute-start | bytes 1572872 | tf_op jit(solution)/shard_map/ppermute | solution.py:19
  201.3 1.5 broadcast_in_dim.10
  202.8 0.8 constant_dynamic-update-slice_fusion.3
  203.6 1.1 copy.42
  204.8 1.9 constant_dynamic-update-slice_fusion.2
  206.6 1.9 constant_dynamic-update-slice_fusion.1
  208.5 4.1 collective-permute-done.2
  212.6 1.9 constant_dynamic-update-slice_fusion
  214.5 2.4 fusion.34
  216.9 2.0 copy-done.2
  218.9 1.1 fusion.50
  220.0 3.9 copy.28
  223.9 5.9 %fusion.27 = f32[16,128,128]{1,2,0:T(8,128)S(1)} fusion(bf16[512,16,128]{0,2,1:T(8,128)(2,1)} %bitcast.92, f32[16,128]{1,0:T(8,128)S(1)} %fusion.50, f32[16,512,128]{2,1,0:T(8,128)} %copy-done.2), kind=kOutput, calls=%fused_computation.39 | convolution fusion | flops 273680896 | bytes 7348224 | tf_op jit(solution)/shard_map/hqk,khd->qhd/dot_general | solution.py:43
  229.8 1.3 copy.36
  231.1 1.5 fusion.30
  232.8 1.0 fusion.33
  233.8 9.6 %scatter_custom_fusion = bf16[1088,2048]{1,0:T(8,128)(2,1)} fusion(s32[1024]{0:T(1024)S(1)} %bitcast.99, bf16[]{:T(256)} %constant.46.clone.1, bf16[128,2048]{1,0:T(8,128)(2,1)} %fusion.33), kind=kCustom, calls=%fused_computation.11 | custom fusion | bytes 4980738 | tf_op jit(solution)/shard_map/scatter | solution.py:74
  243.4 7.0 %reshape.110 = bf16[16,68,2048]{2,1,0:T(8,128)(2,1)} reshape(bf16[1088,2048]{1,0:T(8,128)(2,1)} %scatter_custom_fusion) | data formatting | bytes 8912896 | tf_op jit(solution)/shard_map/reshape | solution.py:132
  250.5 6.8 %all-to-all-start = ((bf16[16,68,2048]{2,1,0:T(8,128)(2,1)}), bf16[16,68,2048]{2,1,0:T(8,128)(2,1)}, u32[]{:S(2)}, u32[]{:S(2)}) async-start(bf16[16,68,2048]{2,1,0:T(8,128)(2,1)} %reshape.110), calls=%async_computation | async-start | bytes 9437184 | tf_op jit(solution)/shard_map/all_to_all | solution.py:131
  257.6 7.1 %reshape.113 = bf16[1088,2048]{1,0:T(8,128)(2,1)} reshape(bf16[16,68,2048]{2,1,0:T(8,128)(2,1)} %all-to-all-done.1) | data formatting | bytes 8912896 | tf_op jit(solution)/shard_map/reshape | solution.py:139
  264.6 79.5 %all-to-all-done = bf16[16,68,2048]{2,1,0:T(8,128)(2,1)} async-done(((bf16[16,68,2048]{2,1,0:T(8,128)(2,1)}), bf16[16,68,2048]{2,1,0:T(8,128)(2,1)}, u32[]{:S(2)}, u32[]{:S(2)}) %all-to-all-start) | async-done | bytes 4456480 | tf_op jit(solution)/shard_map/all_to_all | solution.py:131
  344.1 7.1 %reshape.111 = bf16[1088,2048]{1,0:T(8,128)(2,1)} reshape(bf16[16,68,2048]{2,1,0:T(8,128)(2,1)} %all-to-all-done) | data formatting | bytes 8912896 | tf_op jit(solution)/shard_map/reshape | solution.py:138
  351.2 8.0 %fusion.5 = f32[1088,1024]{1,0:T(8,128)S(1)} fusion(bf16[1088,2048]{1,0:T(8,128)(2,1)} %reshape.111, bf16[1,2048,1024]{2,1,0:T(8,128)(2,1)} %param.20), kind=kOutput, calls=%fused_computation.9 | convolution fusion | flops 4563402752 | bytes 13107200 | tf_op jit(solution)/shard_map/dot_general | solution.py:79
  359.2 4.3 convolution_convert_fusion.1
  363.6 3.3 multiply_convert_fusion.2
  366.9 6.2 %convolution_convert_fusion = bf16[2048,1024]{0,1:T(8,128)(2,1)S(1)} fusion(bf16[1088,2048]{1,0:T(8,128)(2,1)S(1)} %bitcast.89, bf16[1088,512]{1,0:T(8,128)(2,1)S(1)} %get-tuple-element.10, bf16[1088,512]{1,0:T(8,128)(2,1)S(1)} %get-tuple-element.9), kind=kOutput, calls=%fused_computation.21 | convolution fusion | flops 4569956352 | bytes 10878976 | tf_op jit(solution)/shard_map/dot_general | solution.py:95
  373.1 3.7 pad_maximum_fusion
  377.2 0.7 copy-done.4
  377.9 0.9 fusion.28
  378.8 92.4 %reduce-scatter.2.cloned.1.call-done = bf16[1024,1536]{0,1:T(8,128)(2,1)} async-done(((bf16[2048,1536]{0,1:T(8,128)(2,1)}), bf16[1024,1536]{0,1:T(8,128)(2,1)}) %reduce-scatter.2.cloned.1.call-update) | async-done | bytes 3145744 | tf_op jit(solution)/shard_map/reduce_scatter | solution.py:141
  471.2 2.6 convert_element_type.76
  473.8 1.6 slice_bitcast_fusion.1
  475.4 2.5 slice_bitcast_fusion
  477.9 5.5 %copy.38 = f32[1,1024,1024]{2,1,0:T(8,128)} copy(f32[1,1024,1024]{1,2,0:T(8,128)} %slice_bitcast_fusion) | data formatting | bytes 8388608
  483.4 2.9 copy.39
  (48 shorter events, 2.3 us)
Async XLA Ops:
  7.2 356.4 %copy-start = (bf16[1,2048,512]{2,1,0:T(8,128)(2,1)S(1)}, bf16[1,2048,512]{2,1,0:T(8,128)(2,1)}, u32[]{:S(2)}) copy-start(bf16[1,2048,512]{2,1,0:T(8,128)(2,1)} %param.21) | copy-start | bytes 6291460
  33.8 8.3 %copy-start.5 = (bf16[1,128,2048]{2,1,0:T(8,128)(2,1)S(1)}, bf16[1,128,2048]{2,1,0:T(8,128)(2,1)}, u32[]{:S(2)}) copy-start(bf16[1,128,2048]{2,1,0:T(8,128)(2,1)} %param.12) | copy-start | bytes 1572868
  33.8 216.7 %all-to-all-start.1 = ((bf16[16,68,2048]{2,1,0:T(8,128)(2,1)}), bf16[16,68,2048]{2,1,0:T(8,128)(2,1)}, u32[]{:S(2)}, u32[]{:S(2)}) async-start(bf16[16,68,2048]{2,1,0:T(8,128)(2,1)} %reshape.112), calls=%async_computation.1 | async-start | bytes 9437184 | tf_op jit(solution)/shard_map/all_to_all | solution.py:134
  41.3 178.6 %all-gather.2.cloned.1.call-start = ((), (), s32[]{:S(2)}) async-start(), calls=%async_computation.3 | async-start | bytes 2621440 | tf_op jit(solution)/shard_map/all_gather | solution.py:115
  42.4 125.4 %collective-permute-start = (bf16[1,128,2048]{1,2,0:T(8,128)(2,1)S(1)}, bf16[1,128,2048]{1,2,0:T(8,128)(2,1)}, u32[]{:S(2)}, u32[]{:S(2)}) collective-permute-start(bf16[1,128,2048]{1,2,0:T(8,128)(2,1)S(1)} %copy.23), channel_id=1, source_target_pairs={{0,4},{4,8},{8,12},{12,0},{1,5},{5,9},{9,13},{13,1},{2,6},{6,10},{... | collective-permute-start | bytes 1572872 | tf_op jit(solution)/shard_map/ppermute | solution.py:19
  44.3 162.3 %collective-permute-start.1 = (bf16[1,128,2048]{1,2,0:T(8,128)(2,1)S(1)}, bf16[1,128,2048]{1,2,0:T(8,128)(2,1)}, u32[]{:S(2)}, u32[]{:S(2)}) collective-permute-start(bf16[1,128,2048]{1,2,0:T(8,128)(2,1)S(1)} %copy.23), channel_id=1, source_target_pairs={{0,12},{4,0},{8,4},{12,8},{1,13},{5,1},{9,5},{13,9},{2,14},{6,2},{... | collective-permute-start | bytes 1572872 | tf_op jit(solution)/shard_map/ppermute | solution.py:22
  167.8 44.8 %collective-permute-start.2 = (bf16[1,128,2048]{1,2,0:T(8,128)(2,1)}, bf16[1,128,2048]{1,2,0:T(8,128)(2,1)}, u32[]{:S(2)}, u32[]{:S(2)}) collective-permute-start(bf16[1,128,2048]{1,2,0:T(8,128)(2,1)} %collective-permute-done), channel_id=1, source_target_pairs={{0,4},{4,8},{8,12},{12,0},{1,5},{5,9},{9,13},{13,1},{2,6},{6,10},{... | collective-permute-start | bytes 1572872 | tf_op jit(solution)/shard_map/ppermute | solution.py:19
  216.9 2.0 copy-start.2
  229.8 3.0 copy-start.6
  250.5 93.6 %all-to-all-start = ((bf16[16,68,2048]{2,1,0:T(8,128)(2,1)}), bf16[16,68,2048]{2,1,0:T(8,128)(2,1)}, u32[]{:S(2)}, u32[]{:S(2)}) async-start(bf16[16,68,2048]{2,1,0:T(8,128)(2,1)} %reshape.110), calls=%async_computation | async-start | bytes 9437184 | tf_op jit(solution)/shard_map/all_to_all | solution.py:131
  257.3 213.9 %reduce-scatter.2.cloned.1.call-start = ((), (), s32[]{:S(2)}) async-start(), calls=%async_computation.4 | async-start | bytes 9437184 | tf_op jit(solution)/shard_map/reduce_scatter | solution.py:141
  344.1 15.1 %slice-start = ((s8[4456448]{0:T(1024)(128)(4,1)}), s8[262144]{0:T(1024)(128)(4,1)S(1)}, s32[]{:S(2)}) async-start(s8[4456448]{0:T(1024)(128)(4,1)} %bitcast.86), calls=%async_computation.5 | async-start | bytes 524288
  351.2 8.0 %slice-start.1 = ((s8[4456448]{0:T(1024)(128)(4,1)}), s8[4194304]{0:T(1024)(128)(4,1)S(1)}, s32[]{:S(2)}) async-start(s8[4456448]{0:T(1024)(128)(4,1)} %bitcast.86), calls=%async_computation.6 | async-start | bytes 8388608
  359.2 7.7 %slice-start.2 = ((s8[4456448]{0:T(1024)(128)(4,1)}), s8[4194304]{0:T(1024)(128)(4,1)S(1)}, s32[]{:S(2)}) async-start(s8[4456448]{0:T(1024)(128)(4,1)} %bitcast.88), calls=%async_computation.7 | async-start | bytes 8388608
  363.6 3.3 slice-start.3
  366.9 6.3 %copy-start.3 = (bf16[2048,512]{0,1:T(8,128)(2,1)S(1)}, bf16[2048,512]{0,1:T(8,128)(2,1)}, u32[]{:S(2)}) copy-start(bf16[2048,512]{0,1:T(8,128)(2,1)} %convolution_convert_fusion.1) | copy-start | bytes 6291460
  376.9 1.0 copy-start.4
  477.9 8.4 %copy-start.1 = (bf16[1,2048,512]{2,1,0:T(8,128)(2,1)S(1)}, bf16[1,2048,512]{2,1,0:T(8,128)(2,1)}, u32[]{:S(2)}) copy-start(bf16[1,2048,512]{2,1,0:T(8,128)(2,1)} %param.21) | copy-start | bytes 6291460
Sparse Core Ops, SparseCore 0:
  43.8 104.0 all-gather.1
  377.0 94.1 reduce-scatter.1
